TPU v7x, 32 devices: a whole 2x2x4 slice. The times are simulated.
32 devices in a mesh: row: 8 (over z, y), col: 4 (over x, core).
Axes of the slice: x: 2, y: 2, z: 4, core: 2. Of those that a mesh axis runs over, the one named last changes fastest.
Arguments:
- error: float32 [14336, 16384], P('row', 'col'), may hold values from -0.046875 to 0.046875
- covar: float32 [16384, 16384], P('row', 'col'), may hold values from -1 to 6, as said below
- basis: float32 [14336, 128], P('row'), may hold values from -6 to 6
Outputs:
- new_basis: float32 [14336, 128], P('row')
- factor: float32 [128, 128], replicated
Inputs may be any that keep to these rules, and one draw needn't show every extreme that they name: covar is symmetric and positive definite.
All inputs are finite; a program needn't handle non-finite values.
Results may differ from a plain program's by a relative error of at most 0.0001.
Values sent between devices are 32-bit elements; how exact they have to be, the bound alone decides.
A program may use at most 128 MiB of HBM per device.

v0:
```python
import jax
import jax.numpy as jnp
from jax import lax
from jax.sharding import PartitionSpec as P

ITERS = 2


def local(error, covar, basis):
    high = lax.Precision.HIGHEST
    col_width = error.shape[1]
    rows_all = error.shape[0] * lax.axis_size("row")
    current = basis
    lower = jnp.zeros((basis.shape[1], basis.shape[1]), jnp.float32)
    for step in range(ITERS):
        partial_proj = lax.dot_general(
            error,
            current,
            (((0,), (0,)), ((), ())),
            precision=high,
            preferred_element_type=jnp.float32,
        )
        projected = lax.psum(partial_proj, "row")
        image_part = jnp.dot(covar, projected, precision=high, preferred_element_type=jnp.float32)
        image_share = lax.psum_scatter(image_part, "col", scatter_dimension=0, tiled=True)
        whole = lax.all_gather(image_share, ("row", "col"), axis=0, tiled=True)
        needed = lax.dynamic_slice_in_dim(whole, lax.axis_index("col") * col_width, col_width, 0)
        block_part = jnp.dot(error, needed, precision=high, preferred_element_type=jnp.float32)
        block = lax.psum(block_part, "col")
        local_gram = jnp.dot(block.T, block, precision=high, preferred_element_type=jnp.float32)
        gram = lax.psum(local_gram, "row") / rows_all
        lower = jnp.linalg.cholesky(gram)
        current = lax.linalg.triangular_solve(
            lower, block, left_side=False, lower=True, transpose_a=True
        )
    return (current, lower.T)


def solution(mesh):
    in_specs = (P("row", "col"), P("row", "col"), P("row", None))
    out_specs = (P("row", None), P())
    return jax.shard_map(local, mesh=mesh, in_specs=in_specs, out_specs=out_specs, check_vma=False)
```

profile of v0, /device:TPU:0, one launch (start us, length us, event | category | flops | bytes accessed | tf_op | source)
XLA Modules:
  0.0 928.3 jit_solution(5317270569974142833)
XLA Ops:
  7.2 0.0 copy-start
  7.2 0.0 all-reduce.7.cloned.1.call-start
  7.2 1.1 copy-done
  8.4 50.0 %fusion.13 = f32[4096,128]{1,0:T(8,128)} fusion(f32[1792,4096]{1,0:T(8,128)} %param.6, f32[1792,128]{1,0:T(8,128)S(1)} %copy-done), kind=kOutput, calls=%fused_computation.31 | convolution fusion | flops 11274289152 | bytes 32374784 | tf_op jit(solution)/shard_map/dot_general | solution.py:16
  58.3 0.0 all-reduce.7.cloned.1.call-update
  58.4 0.0 reduce-scatter.3.cloned.1.call-start
  58.4 105.1 %all-reduce.7.cloned.1.call-done = f32[4096,128]{1,0:T(8,128)} async-done(((f32[4096,128]{1,0:T(8,128)}), f32[4096,128]{1,0:T(8,128)}) %all-reduce.7.cloned.1.call-update) | async-done | bytes 2097168 | tf_op jit(solution)/shard_map/psum | solution.py:23
  163.5 42.7 %convolution_bitcast_fusion.2 = f32[2048,128]{0,1:T(8,128)} fusion(f32[4096,128]{1,0:T(8,128)} %all-reduce.7.cloned.1.call-done, f32[2048,4096]{1,0:T(8,128)} %param.7), kind=kOutput, calls=%fused_computation.2 | convolution fusion | flops 12884901888 | bytes 36700160 | tf_op jit(solution)/shard_map/dot_general | solution.py:24
  206.2 0.0 reduce-scatter.3.cloned.1.call-update
  206.2 0.0 all-gather.3.cloned.1.call-start
  206.3 24.2 %reduce-scatter.3.cloned.1.call-done = f32[512,128]{0,1:T(8,128)} async-done(((f32[2048,128]{0,1:T(8,128)}), f32[512,128]{0,1:T(8,128)}) %reduce-scatter.3.cloned.1.call-update) | async-done | bytes 262160 | tf_op jit(solution)/shard_map/reduce_scatter | solution.py:25
  230.5 0.0 all-gather.3.cloned.1.call-update
  230.5 0.0 all-reduce.9.cloned.1.call-start
  230.5 80.3 %all-gather.3.cloned.1.call-done = f32[16384,128]{0,1:T(8,128)} async-done(((f32[512,128]{0,1:T(8,128)}), f32[16384,128]{0,1:T(8,128)}) %all-gather.3.cloned.1.call-update) | async-done | bytes 8388624 | tf_op jit(solution)/shard_map/all_gather | solution.py:26
  310.8 34.1 %convolution_bitcast_fusion.6 = f32[1792,128]{0,1:T(8,128)} fusion(f32[1792,4096]{1,0:T(8,128)} %param.6, f32[16384,128]{0,1:T(8,128)} %all-gather.3.cloned.1.call-done, s32[]{:T(128)S(6)} %select_n.7), kind=kOutput, calls=%fused_computation.6 | convolution fusion | flops 11274289152 | bytes 32374788 | tf_op jit(solution)/shard_map/dot_general | solution.py:28
  345.0 0.0 all-reduce.9.cloned.1.call-update
  345.0 0.0 all-reduce.11.cloned.1.call-start
  345.1 35.2 %all-reduce.9.cloned.1.call-done = f32[1792,128]{0,1:T(8,128)} async-done(((f32[1792,128]{0,1:T(8,128)}), f32[1792,128]{0,1:T(8,128)}) %all-reduce.9.cloned.1.call-update) | async-done | bytes 917520 | tf_op jit(solution)/shard_map/psum | solution.py:29
  380.2 3.0 fusion.14
  383.2 0.0 all-reduce.11.cloned.1.call-update
  383.2 0.0 all-reduce.13.cloned.1.call-start
  383.3 70.2 %all-reduce.11.cloned.1.call-done = f32[128,128]{0,1:T(8,128)} async-done(((f32[128,128]{0,1:T(8,128)}), f32[128,128]{0,1:T(8,128)}) %all-reduce.11.cloned.1.call-update) | async-done | bytes 65552 | tf_op jit(solution)/shard_map/psum | solution.py:31
  453.5 0.8 broadcast_multiply_fusion.1
  454.3 0.1 copy.6
  454.4 0.9 fusion.6
  455.3 11.7 %cholesky.44 = f32[128,128]{1,0:T(8,128)S(1)} custom-call(f32[128,128]{1,0:T(8,128)S(1)} %fusion.6), custom_call_target="Cholesky" | custom-call | tf_op jit(solution)/shard_map/jit(cholesky)/cholesky | solution.py:32
  467.0 0.6 compare_reduce_fusion.1
  467.7 0.7 fusion.2
  468.3 9.8 %custom-call.6 = f32[1,128,128]{1,2,0:T(8,128)S(1)} custom-call(f32[1,128,128]{2,1,0:T(8,128)S(1)} %fusion.2), custom_call_target="InvertDiagBlocksLowerTriangular" | custom-call | tf_op jit(solution)/shard_map/triangular_solve/custom-call.0 | solution.py:33
  478.1 2.1 convolution_bitcast_fusion.4
  480.3 22.0 %convolution_bitcast_fusion = f32[4096,128]{0,1:T(8,128)} fusion(f32[1792,128]{0,1:T(8,128)S(1)} %convolution_bitcast_fusion.4, f32[1792,4096]{1,0:T(8,128)} %param.6), kind=kOutput, calls=%fused_computation | convolution fusion | flops 11274289152 | bytes 32374784 | tf_op jit(solution)/shard_map/dot_general | solution.py:16
  502.2 0.0 all-reduce.13.cloned.1.call-update
  502.3 0.0 reduce-scatter.5.cloned.1.call-start
  502.3 102.4 %all-reduce.13.cloned.1.call-done = f32[4096,128]{0,1:T(8,128)} async-done(((f32[4096,128]{0,1:T(8,128)}), f32[4096,128]{0,1:T(8,128)}) %all-reduce.13.cloned.1.call-update) | async-done | bytes 2097168 | tf_op jit(solution)/shard_map/psum | solution.py:23
  604.7 40.1 %convolution_bitcast_fusion.1 = f32[2048,128]{0,1:T(8,128)} fusion(f32[4096,128]{0,1:T(8,128)} %all-reduce.13.cloned.1.call-done, f32[2048,4096]{1,0:T(8,128)} %param.7), kind=kOutput, calls=%fused_computation.1 | convolution fusion | flops 12884901888 | bytes 36700160 | tf_op jit(solution)/shard_map/dot_general | solution.py:24
  644.8 0.0 reduce-scatter.5.cloned.1.call-update
  644.8 0.0 all-gather.5.cloned.1.call-start
  644.8 24.2 %reduce-scatter.5.cloned.1.call-done = f32[512,128]{0,1:T(8,128)} async-done(((f32[2048,128]{0,1:T(8,128)}), f32[512,128]{0,1:T(8,128)}) %reduce-scatter.5.cloned.1.call-update) | async-done | bytes 262160 | tf_op jit(solution)/shard_map/reduce_scatter | solution.py:25
  669.0 0.0 all-gather.5.cloned.1.call-update
  669.0 0.0 all-reduce.15.cloned.1.call-start
  669.1 80.3 %all-gather.5.cloned.1.call-done = f32[16384,128]{0,1:T(8,128)} async-done(((f32[512,128]{0,1:T(8,128)}), f32[16384,128]{0,1:T(8,128)}) %all-gather.5.cloned.1.call-update) | async-done | bytes 8388624 | tf_op jit(solution)/shard_map/all_gather | solution.py:26
  749.4 0.0 copy-start.1
  749.4 34.6 %convolution_bitcast_fusion.5 = f32[1792,128]{0,1:T(8,128)} fusion(f32[1792,4096]{1,0:T(8,128)} %param.6, f32[16384,128]{0,1:T(8,128)} %all-gather.5.cloned.1.call-done, s32[]{:T(128)S(6)} %select_n.7), kind=kOutput, calls=%fused_computation.5 | convolution fusion | flops 11274289152 | bytes 32374788 | tf_op jit(solution)/shard_map/dot_general | solution.py:28
  784.0 0.0 all-reduce.15.cloned.1.call-update
  784.0 0.2 all-reduce.17.cloned.1.call-start
  784.2 35.0 %all-reduce.15.cloned.1.call-done = f32[1792,128]{0,1:T(8,128)} async-done(((f32[1792,128]{0,1:T(8,128)}), f32[1792,128]{0,1:T(8,128)}) %all-reduce.15.cloned.1.call-update) | async-done | bytes 917520 | tf_op jit(solution)/shard_map/psum | solution.py:29
  819.3 3.0 fusion.15
  822.2 0.0 all-reduce.17.cloned.1.call-update
  822.3 70.3 %all-reduce.17.cloned.1.call-done = f32[128,128]{0,1:T(8,128)} async-done(((f32[128,128]{0,1:T(8,128)}), f32[128,128]{0,1:T(8,128)}) %all-reduce.17.cloned.1.call-update) | async-done | bytes 65552 | tf_op jit(solution)/shard_map/psum | solution.py:31
  892.5 0.8 broadcast_multiply_fusion
  893.4 0.1 copy.8
  893.5 0.9 fusion.4
  894.3 11.7 %cholesky.55 = f32[128,128]{1,0:T(8,128)S(1)} custom-call(f32[128,128]{1,0:T(8,128)S(1)} %fusion.4), custom_call_target="Cholesky" | custom-call | tf_op jit(solution)/shard_map/jit(cholesky)/cholesky | solution.py:32
  906.1 0.6 compare_reduce_fusion
  906.7 0.7 fusion.10
  907.4 0.7 copy.10
  908.1 9.8 %custom-call.7 = f32[1,128,128]{1,2,0:T(8,128)S(1)} custom-call(f32[1,128,128]{2,1,0:T(8,128)S(1)} %get-tuple-element.7), custom_call_target="InvertDiagBlocksLowerTriangular" | custom-call | tf_op jit(solution)/shard_map/triangular_solve/custom-call.0 | solution.py:33
  917.9 2.1 convolution_bitcast_fusion.3
  920.0 1.2 copy.9
  921.3 0.0 copy-done.1
  (2 shorter events, 0.1 us)
Async XLA Ops:
  7.2 1.2 copy-start
  7.2 156.4 %all-reduce.7.cloned.1.call-start = ((), (), s32[]{:S(2)}) async-start(), calls=%async_computation.2 | async-start | bytes 4194304 | tf_op jit(solution)/shard_map/psum | solution.py:23
  58.4 172.1 %reduce-scatter.3.cloned.1.call-start = ((), (), s32[]{:S(2)}) async-start(), calls=%async_computation.3 | async-start | bytes 1310720 | tf_op jit(solution)/shard_map/reduce_scatter | solution.py:25
  206.2 104.6 %all-gather.3.cloned.1.call-start = ((), (), s32[]{:S(2)}) async-start(), calls=%async_computation.4 | async-start | bytes 8650752 | tf_op jit(solution)/shard_map/all_gather | solution.py:26
  230.5 149.7 %all-reduce.9.cloned.1.call-start = ((), (), s32[]{:S(2)}) async-start(), calls=%async_computation.5 | async-start | bytes 1835008 | tf_op jit(solution)/shard_map/psum | solution.py:29
  345.0 108.5 %all-reduce.11.cloned.1.call-start = ((), (), s32[]{:S(2)}) async-start(), calls=%async_computation.6 | async-start | bytes 131072 | tf_op jit(solution)/shard_map/psum | solution.py:31
  383.2 221.5 %all-reduce.13.cloned.1.call-start = ((), (), s32[]{:S(2)}) async-start(), calls=%async_computation.7 | async-start | bytes 4194304 | tf_op jit(solution)/shard_map/psum | solution.py:23
  502.3 166.7 %reduce-scatter.5.cloned.1.call-start = ((), (), s32[]{:S(2)}) async-start(), calls=%async_computation.8 | async-start | bytes 1310720 | tf_op jit(solution)/shard_map/reduce_scatter | solution.py:25
  644.8 104.6 %all-gather.5.cloned.1.call-start = ((), (), s32[]{:S(2)}) async-start(), calls=%async_computation.9 | async-start | bytes 8650752 | tf_op jit(solution)/shard_map/all_gather | solution.py:26
  669.0 150.2 %all-reduce.15.cloned.1.call-start = ((), (), s32[]{:S(2)}) async-start(), calls=%async_computation.10 | async-start | bytes 1835008 | tf_op jit(solution)/shard_map/psum | solution.py:29
  749.4 171.9 %copy-start.1 = (f32[1792,128]{1,0:T(8,128)S(1)}, f32[1792,128]{1,0:T(8,128)}, u32[]{:S(2)}) copy-start(f32[1792,128]{1,0:T(8,128)} %param.8) | copy-start | bytes 2752516
  784.0 108.5 %all-reduce.17.cloned.1.call-start = ((), (), s32[]{:S(2)}) async-start(), calls=%async_computation.11 | async-start | bytes 131072 | tf_op jit(solution)/shard_map/psum | solution.py:31
Sparse Core Ops, SparseCore 0:
  58.5 105.0 all-reduce.6
  206.4 24.0 reduce-scatter.2
  233.4 77.4 all-gather.2
  345.1 35.0 all-reduce.8
  384.0 69.3 all-reduce.10
  502.4 102.2 all-reduce.12
  644.9 24.0 reduce-scatter.4
  671.9 77.4 all-gather.4
  784.1 35.0 all-reduce.14
  823.1 69.3 all-reduce.16
where the time goes:
time: 937 us; the launch traced here: 928 us
  waiting for transfers between devices  627 us (67%)
  matrix products  234 us (25%)
  other arithmetic  49.1 us (5%)
  between operations  14.4 us (2%)
    psum x2, waiting for transfers between devices, local(): projected = lax.psum(partial_proj, 'row')  207 us
    all_gather x2, waiting for transfers between devices, local(): whole = lax.all_gather(image_share, ('row', 'col'), axis=0, tiled=True)  161 us
    psum x2, waiting for transfers between devices, local(): gram = lax.psum(local_gram, 'row') / rows_all  140 us
    dot_general x2, matrix products, local(): jnp.dot(covar, projected, precision=high, preferred_element_type=jnp.floa...  82.8 us
    dot_general x2, matrix products, local(): lax.dot_general(error, current, (((0,), (0,)), ((), ())), precision=high,...  71.9 us
    psum x2, waiting for transfers between devices, local(): block = lax.psum(block_part, 'col')  70.2 us
    dot_general x2, matrix products, local(): jnp.dot(error, needed, precision=high, preferred_element_type=jnp.float32)  68.7 us
    reduce_scatter x2, waiting for transfers between devices, local(): lax.psum_scatter(image_part, 'col', scatter_dimension=0, tiled=True)  48.3 us
  transfers between devices with their start and end apart: 10, of which 10 were waited for; matrix products, arithmetic and copies ran while one was open for 0% of the time, Pallas kernels for 0%

commit v1 on v0

--- a/solution.py
+++ b/solution.py
@@ -20,7 +20,8 @@
             precision=high,
             preferred_element_type=jnp.float32,
         )
-        projected = lax.psum(partial_proj, "row")
+        parts = lax.all_gather(partial_proj, "row")
+        projected = jnp.sum(parts, axis=0)
         image_part = jnp.dot(covar, projected, precision=high, preferred_element_type=jnp.float32)
         image_share = lax.psum_scatter(image_part, "col", scatter_dimension=0, tiled=True)
         whole = lax.all_gather(image_share, ("row", "col"), axis=0, tiled=True)

time: 937 us -> 1220 us (1.30)
  waiting for transfers between devices: 627 us -> 875 us
  local copies, waits for them, and re-layouts: 3.27 us -> 18.9 us
    all_gather x0 -> x2, waiting for transfers between devices: none -> 457 us  [local(): parts = lax.all_gather(partial_proj, 'row')]
    psum x2 -> x0, waiting for transfers between devices: 207 us -> none  [local(): projected = lax.psum(partial_proj, 'row')]
    unnamed x6 -> x7, local copies, waits for them, and re-layouts: 3.09 us -> 18.7 us
where the time goes in v1:
time: 1220 us; the launch traced here: 1210 us
  waiting for transfers between devices  875 us (72%)
  matrix products  242 us (20%)
  other arithmetic  61.2 us (5%)
  local copies, waits for them, and re-layouts  18.9 us (2%)
  between operations  14.7 us (1%)
    all_gather x2, waiting for transfers between devices, local(): parts = lax.all_gather(partial_proj, 'row')  457 us
    all_gather x2, waiting for transfers between devices, local(): whole = lax.all_gather(image_share, ('row', 'col'), axis=0, tiled=True)  161 us
    psum x2, waiting for transfers between devices, local(): gram = lax.psum(local_gram, 'row') / rows_all  140 us
    dot_general x2, matrix products, local(): jnp.dot(covar, projected, precision=high, preferred_element_type=jnp.floa...  90.6 us
    dot_general x2, matrix products, local(): lax.dot_general(error, current, (((0,), (0,)), ((), ())), precision=high,...  72.2 us
    psum x2, waiting for transfers between devices, local(): block = lax.psum(block_part, 'col')  70.2 us
    dot_general x2, matrix products, local(): jnp.dot(error, needed, precision=high, preferred_element_type=jnp.float32)  68.5 us
    reduce_scatter x2, waiting for transfers between devices, local(): lax.psum_scatter(image_part, 'col', scatter_dimension=0, tiled=True)  46.2 us
  transfers between devices with their start and end apart: 10, of which 10 were waited for; matrix products, arithmetic and copies ran while one was open for 0% of the time, Pallas kernels for 0%

profile of v1, /device:TPU:0, one launch (start us, length us, event | category | flops | bytes accessed | tf_op | source)
XLA Modules:
  0.0 1211.6 jit_solution(16127180276892198364)
XLA Ops:
  7.2 0.0 copy-start
  7.2 0.0 all-gather.11.cloned.1.call-start
  7.2 1.1 copy-done
  8.4 50.0 %fusion.13 = f32[4096,128]{1,0:T(8,128)} fusion(f32[1792,4096]{1,0:T(8,128)} %param.6, f32[1792,128]{1,0:T(8,128)S(1)} %copy-done), kind=kOutput, calls=%fused_computation.32 | convolution fusion | flops 11274289152 | bytes 32374784 | tf_op jit(solution)/shard_map/dot_general | solution.py:16
  58.3 0.0 all-gather.11.cloned.1.call-update
  58.4 0.0 reduce-scatter.3.cloned.1.call-start
  58.4 230.1 %all-gather.11.cloned.1.call-done = f32[32768,128]{1,0:T(8,128)} async-done(((f32[4096,128]{1,0:T(8,128)}), f32[32768,128]{1,0:T(8,128)}) %all-gather.11.cloned.1.call-update) | async-done | bytes 16777232 | tf_op jit(solution)/shard_map/all_gather | solution.py:23
  288.5 6.8 reduce_sum.18
  295.3 51.8 %convolution_bitcast_fusion.2 = f32[2048,128]{0,1:T(8,128)} fusion(f32[4096,128]{1,0:T(8,128)S(1)} %reduce_sum.18, f32[2048,4096]{1,0:T(8,128)} %param.7), kind=kOutput, calls=%fused_computation.3 | convolution fusion | flops 12884901888 | bytes 36700160 | tf_op jit(solution)/shard_map/dot_general | solution.py:25
  347.1 0.0 reduce-scatter.3.cloned.1.call-update
  347.2 0.0 all-gather.7.cloned.1.call-start
  347.2 23.1 %reduce-scatter.3.cloned.1.call-done = f32[512,128]{0,1:T(8,128)} async-done(((f32[2048,128]{0,1:T(8,128)}), f32[512,128]{0,1:T(8,128)}) %reduce-scatter.3.cloned.1.call-update) | async-done | bytes 262160 | tf_op jit(solution)/shard_map/reduce_scatter | solution.py:26
  370.3 0.0 all-gather.7.cloned.1.call-update
  370.3 0.0 all-reduce.5.cloned.1.call-start
  370.4 80.3 %all-gather.7.cloned.1.call-done = f32[16384,128]{0,1:T(8,128)} async-done(((f32[512,128]{0,1:T(8,128)}), f32[16384,128]{0,1:T(8,128)}) %all-gather.7.cloned.1.call-update) | async-done | bytes 8388624 | tf_op jit(solution)/shard_map/all_gather | solution.py:27
  450.6 34.2 %convolution_bitcast_fusion.6 = f32[1792,128]{0,1:T(8,128)} fusion(f32[1792,4096]{1,0:T(8,128)} %param.6, f32[16384,128]{0,1:T(8,128)} %all-gather.7.cloned.1.call-done, s32[]{:T(128)S(6)} %select_n.7), kind=kOutput, calls=%fused_computation.7 | convolution fusion | flops 11274289152 | bytes 32374788 | tf_op jit(solution)/shard_map/dot_general | solution.py:29
  484.8 0.0 all-reduce.5.cloned.1.call-update
  484.8 0.0 all-reduce.7.cloned.1.call-start
  484.9 35.2 %all-reduce.5.cloned.1.call-done = f32[1792,128]{0,1:T(8,128)} async-done(((f32[1792,128]{0,1:T(8,128)}), f32[1792,128]{0,1:T(8,128)}) %all-reduce.5.cloned.1.call-update) | async-done | bytes 917520 | tf_op jit(solution)/shard_map/psum | solution.py:30
  520.0 3.0 fusion.14
  523.0 0.0 all-reduce.7.cloned.1.call-update
  523.0 0.0 all-gather.13.cloned.1.call-start
  523.1 70.2 %all-reduce.7.cloned.1.call-done = f32[128,128]{0,1:T(8,128)} async-done(((f32[128,128]{0,1:T(8,128)}), f32[128,128]{0,1:T(8,128)}) %all-reduce.7.cloned.1.call-update) | async-done | bytes 65552 | tf_op jit(solution)/shard_map/psum | solution.py:32
  593.3 0.8 broadcast_multiply_fusion.1
  594.2 0.1 copy.12
  594.3 0.9 fusion.6
  595.1 11.7 cholesky.44
  606.9 0.6 compare_reduce_fusion.1
  607.5 0.7 fusion.2
  608.2 9.8 custom-call.6
  618.0 2.1 convolution_bitcast_fusion.4
  620.1 22.2 %convolution_bitcast_fusion = f32[4096,128]{0,1:T(8,128)} fusion(f32[1792,128]{0,1:T(8,128)S(1)} %convolution_bitcast_fusion.4, f32[1792,4096]{1,0:T(8,128)} %param.6), kind=kOutput, calls=%fused_computation.1 | convolution fusion | flops 11274289152 | bytes 32374784 | tf_op jit(solution)/shard_map/dot_general | solution.py:16
  642.3 0.0 all-gather.13.cloned.1.call-update
  642.3 0.0 reduce-scatter.5.cloned.1.call-start
  642.4 227.3 %all-gather.13.cloned.1.call-done = f32[32768,128]{0,1:T(8,128)} async-done(((f32[4096,128]{0,1:T(8,128)}), f32[32768,128]{0,1:T(8,128)}) %all-gather.13.cloned.1.call-update) | async-done | bytes 16777232 | tf_op jit(solution)/shard_map/all_gather | solution.py:23
  869.7 15.6 %copy.19 = f32[16,8,8,4096]{3,2,1,0:T(8,128)S(1)} copy(f32[16,8,8,4096]{3,1,2,0:T(8,128)} %bitcast.57) | data formatting | bytes 33554432
  885.3 5.3 bitcast_reduce_fusion
  890.6 38.8 %convolution_bitcast_fusion.1 = f32[2048,128]{0,1:T(8,128)} fusion(f32[4096,128]{0,1:T(8,128)S(1)} %bitcast_reduce_fusion, f32[2048,4096]{1,0:T(8,128)} %param.7), kind=kOutput, calls=%fused_computation.2 | convolution fusion | flops 12884901888 | bytes 36700160 | tf_op jit(solution)/shard_map/dot_general | solution.py:25
  929.4 0.0 reduce-scatter.5.cloned.1.call-update
  929.5 0.0 all-gather.9.cloned.1.call-start
  929.5 23.1 %reduce-scatter.5.cloned.1.call-done = f32[512,128]{0,1:T(8,128)} async-done(((f32[2048,128]{0,1:T(8,128)}), f32[512,128]{0,1:T(8,128)}) %reduce-scatter.5.cloned.1.call-update) | async-done | bytes 262160 | tf_op jit(solution)/shard_map/reduce_scatter | solution.py:26
  952.6 0.0 all-gather.9.cloned.1.call-update
  952.6 0.0 copy-start.1
  952.6 0.0 all-reduce.9.cloned.1.call-start
  952.7 80.3 %all-gather.9.cloned.1.call-done = f32[16384,128]{0,1:T(8,128)} async-done(((f32[512,128]{0,1:T(8,128)}), f32[16384,128]{0,1:T(8,128)}) %all-gather.9.cloned.1.call-update) | async-done | bytes 8388624 | tf_op jit(solution)/shard_map/all_gather | solution.py:27
  1032.9 34.3 %convolution_bitcast_fusion.5 = f32[1792,128]{0,1:T(8,128)} fusion(f32[1792,4096]{1,0:T(8,128)} %param.6, f32[16384,128]{0,1:T(8,128)} %all-gather.9.cloned.1.call-done, s32[]{:T(128)S(6)} %select_n.7), kind=kOutput, calls=%fused_computation.6 | convolution fusion | flops 11274289152 | bytes 32374788 | tf_op jit(solution)/shard_map/dot_general | solution.py:29
  1067.3 0.0 all-reduce.9.cloned.1.call-update
  1067.3 0.0 all-reduce.11.cloned.1.call-start
  1067.4 35.0 %all-reduce.9.cloned.1.call-done = f32[1792,128]{0,1:T(8,128)} async-done(((f32[1792,128]{0,1:T(8,128)}), f32[1792,128]{0,1:T(8,128)}) %all-reduce.9.cloned.1.call-update) | async-done | bytes 917520 | tf_op jit(solution)/shard_map/psum | solution.py:30
  1102.4 3.0 fusion.15
  1105.4 0.0 all-reduce.11.cloned.1.call-update
  1105.4 70.3 %all-reduce.11.cloned.1.call-done = f32[128,128]{0,1:T(8,128)} async-done(((f32[128,128]{0,1:T(8,128)}), f32[128,128]{0,1:T(8,128)}) %all-reduce.11.cloned.1.call-update) | async-done | bytes 65552 | tf_op jit(solution)/shard_map/psum | solution.py:32
  1175.7 0.8 broadcast_multiply_fusion
  1176.5 0.1 copy.14
  1176.6 0.9 fusion.4
  1177.5 11.7 cholesky.55
  1189.2 0.6 compare_reduce_fusion
  1189.8 0.7 fusion.10
  1190.5 0.7 copy.16
  1191.2 9.8 custom-call.7
  1201.1 2.1 convolution_bitcast_fusion.3
  1203.2 1.2 copy.15
  1204.4 0.0 copy-done.1
  (2 shorter events, 0.1 us)
Async XLA Ops:
  7.2 1.2 copy-start
  7.2 281.3 %all-gather.11.cloned.1.call-start = ((), (), s32[]{:S(2)}) async-start(), calls=%async_computation.10 | async-start | bytes 18874368 | tf_op jit(solution)/shard_map/all_gather | solution.py:23
  58.4 311.9 %reduce-scatter.3.cloned.1.call-start = ((), (), s32[]{:S(2)}) async-start(), calls=%async_computation.2 | async-start | bytes 1310720 | tf_op jit(solution)/shard_map/reduce_scatter | solution.py:26
  347.2 103.5 %all-gather.7.cloned.1.call-start = ((), (), s32[]{:S(2)}) async-start(), calls=%async_computation.3 | async-start | bytes 8650752 | tf_op jit(solution)/shard_map/all_gather | solution.py:27
  370.3 149.7 %all-reduce.5.cloned.1.call-start = ((), (), s32[]{:S(2)}) async-start(), calls=%async_computation.4 | async-start | bytes 1835008 | tf_op jit(solution)/shard_map/psum | solution.py:30
  484.8 108.5 %all-reduce.7.cloned.1.call-start = ((), (), s32[]{:S(2)}) async-start(), calls=%async_computation.5 | async-start | bytes 131072 | tf_op jit(solution)/shard_map/psum | solution.py:32
  523.0 346.7 %all-gather.13.cloned.1.call-start = ((), (), s32[]{:S(2)}) async-start(), calls=%async_computation.11 | async-start | bytes 18874368 | tf_op jit(solution)/shard_map/all_gather | solution.py:23
  642.3 310.2 %reduce-scatter.5.cloned.1.call-start = ((), (), s32[]{:S(2)}) async-start(), calls=%async_computation.6 | async-start | bytes 1310720 | tf_op jit(solution)/shard_map/reduce_scatter | solution.py:26
  929.5 103.5 %all-gather.9.cloned.1.call-start = ((), (), s32[]{:S(2)}) async-start(), calls=%async_computation.7 | async-start | bytes 8650752 | tf_op jit(solution)/shard_map/all_gather | solution.py:27
  952.6 251.8 %copy-start.1 = (f32[1792,128]{1,0:T(8,128)S(1)}, f32[1792,128]{1,0:T(8,128)}, u32[]{:S(2)}) copy-start(f32[1792,128]{1,0:T(8,128)} %param.8) | copy-start | bytes 2752516
  952.6 149.8 %all-reduce.9.cloned.1.call-start = ((), (), s32[]{:S(2)}) async-start(), calls=%async_computation.8 | async-start | bytes 1835008 | tf_op jit(solution)/shard_map/psum | solution.py:30
  1067.3 108.3 %all-reduce.11.cloned.1.call-start = ((), (), s32[]{:S(2)}) async-start(), calls=%async_computation.9 | async-start | bytes 131072 | tf_op jit(solution)/shard_map/psum | solution.py:32
Sparse Core Ops, SparseCore 0:
  58.5 230.0 all-gather.10
  347.3 22.9 reduce-scatter.2
  373.2 77.3 all-gather.6
  484.9 35.0 all-reduce.4
  523.9 69.3 all-reduce.6
  642.5 227.1 all-gather.12
  929.6 22.9 reduce-scatter.4
  955.5 77.3 all-gather.8
  1067.4 34.9 all-reduce.8
  1106.2 69.3 all-reduce.10
